TPU v7x, 32 devices: a whole 2x2x4 slice. The times are simulated.
32 devices in a mesh: group: 2 (over y), src: 4 (over z), rcv: 4 (over x, core).
Axes of the slice: x: 2, y: 2, z: 4, core: 2. Of those that a mesh axis runs over, the one named last changes fastest.
Arguments:
- traces: bfloat16 [128, 36864], P(('group', 'src', 'rcv')), parts along dimension 0, may hold values from -6 to 6
- offsets: int32 [16], P('group'), parts along dimension 0, may hold values from 0 to 32768
- receiver_slots: int32 [8, 16], P(('group', 'rcv')), parts along dimension 0, may hold values from 0 to 15, each once within a row
Outputs:
- correlations: bfloat16 [128, 64, 128], P(('group', 'src'), 'rcv'), parts along dimension 0
There are 2 independent parts, one for each index of `group`. A program takes and returns all parts, laid end to end along the dimension named above; each array names one. Nothing has to cross between parts.
All inputs are finite; a program needn't handle non-finite values.
Results may differ from a plain program's by a relative error of at most 0.0065.
Values may be sent and summed in bfloat16 or wider, within the bound.
No kernel may reach another device: no remote copies, remote signals or barrier semaphores. Data moves between devices by JAX's collectives and lax.ppermute only.
A program may use at most 64 MiB of HBM per device.

v0:
```python
import math
import jax
import jax.numpy as jnp
from jax import lax
from jax.sharding import PartitionSpec as P

SEG_LEN = 4096
NB = 512
LAGS = 128
LAG_STEP = 4
SEGS = 8


def dft_table():
    t_index = jnp.arange(SEG_LEN, dtype=jnp.int32)[:, None]
    k_index = jnp.arange(NB, dtype=jnp.int32)[None, :]
    phase = jnp.mod(t_index * k_index, SEG_LEN).astype(jnp.float32) * (2.0 * math.pi / SEG_LEN)
    return jnp.concatenate([jnp.cos(phase), -jnp.sin(phase)], axis=1).astype(jnp.bfloat16)


def lag_table():
    k_index = jnp.arange(NB, dtype=jnp.int32)[:, None]
    lag_shift = LAG_STEP * (jnp.arange(LAGS, dtype=jnp.int32)[None, :] - LAGS // 2)
    phase = jnp.mod(k_index * lag_shift, SEG_LEN).astype(jnp.float32) * (2.0 * math.pi / SEG_LEN)
    return jnp.concatenate([jnp.cos(phase), -jnp.sin(phase)], axis=0).astype(jnp.bfloat16)


def whiten(traces, offsets):
    table = dft_table()
    pieces = jax.vmap(lambda start: lax.dynamic_slice_in_dim(traces, start, SEG_LEN, 1))(offsets)
    pieces = jnp.transpose(pieces, (1, 0, 2)).reshape(-1, SEG_LEN)
    spectra = jnp.dot(pieces, table, preferred_element_type=jnp.float32)
    energy = jnp.mean(spectra * spectra, axis=-1, keepdims=True)
    white = (spectra / jnp.sqrt(energy + 1e-06)).astype(jnp.bfloat16)
    return white.reshape(traces.shape[0], SEGS, 2 * NB)


def four_sources(sources, receivers, lags):
    src_re = sources[..., :NB]
    src_im = sources[..., NB:]
    rec_re = receivers[..., :NB]
    rec_im = receivers[..., NB:]

    def pair(left, right):
        return jnp.einsum("sgk,rgk->srk", left, right, preferred_element_type=jnp.float32)

    real_part = pair(src_re, rec_re) + pair(src_im, rec_im)
    imag_part = pair(src_re, rec_im) - pair(src_im, rec_re)
    cross = jnp.concatenate([real_part, imag_part], axis=-1).astype(jnp.bfloat16)
    out = jnp.einsum("srk,kl->srl", cross, lags, preferred_element_type=jnp.float32)
    return (out * (1.0 / math.sqrt(SEGS * NB))).astype(jnp.bfloat16)


def correlate(sources, receivers, lags):
    src_count = sources.shape[0]
    grouped = sources.reshape(src_count // 4, 4, SEGS, 2 * NB)
    out = lax.map(lambda blk: four_sources(blk, receivers, lags), grouped)
    return out.reshape(src_count, receivers.shape[0], LAGS)


def on_device(traces, offsets, receiver_slots):
    white = whiten(traces, offsets)
    lags = lag_table()
    sources = lax.all_gather(white, "rcv", axis=0, tiled=True)
    block = correlate(sources, lax.all_gather(white, "src", axis=0, tiled=True), lags)
    return jnp.take(block, receiver_slots[0], axis=1)


def solution(mesh):
    in_specs = (P(("group", "src", "rcv"), None), P("group"), P(("group", "rcv"), None))
    out_specs = P(("group", "src"), "rcv", None)
    return jax.shard_map(
        on_device, mesh=mesh, in_specs=in_specs, out_specs=out_specs, check_vma=False
    )
```

profile of v0, /device:TPU:0, one launch (start us, length us, event | category | flops | bytes accessed | tf_op | source)
XLA Modules:
  0.0 121.1 jit_solution(13736536514290017647)
XLA Ops:
  0.0 0.7 fusion.40
  0.7 16.2 %while.12 = (s32[]{:T(128)}, bf16[4,36864]{1,0:T(4,128)(2,1)}, s32[8,2]{0,1:T(2,128)S(1)}, bf16[8,4,4096]{2,1,0:T(4,128)(2,1)S(1)}, s32[]{:T(128)}) while((s32[]{:T(128)}, bf16[4,36864]{1,0:T(4,128)(2,1)}, s32[8,2]{0,1:T(2,128)S(1)}, bf16[8,4,4096]{2,1,0:T(4,128)(2,1)S(1)}, s32[]{:T(128)}) %tuple.34), condition=%wide.while_cond, body=%wide.while_body.sunk | while | flops 2 | bytes 65633 | solution.py:30
  1.3 1.4 %bitcast_dynamic-update-slice_fusion.2 = bf16[8,4,4096]{2,1,0:T(4,128)(2,1)S(1)} fusion(bf16[8,4,4096]{2,1,0:T(4,128)(2,1)S(1)} %get-tuple-element.139, s32[]{:T(128)} %get-tuple-element.136, bf16[4,36864]{1,0:T(4,128)(2,1)} %get-tuple-element.142, s32[]{:T(128)} %bitcast.79), kind=kLoop, calls=%fused_computation.27.clone.1 | loop fusion | bytes 65544 | tf_op jit(solution)/shard_map/vmap()/gather
  3.3 1.4 %bitcast_dynamic-update-slice_fusion.2 = bf16[8,4,4096]{2,1,0:T(4,128)(2,1)S(1)} fusion(bf16[8,4,4096]{2,1,0:T(4,128)(2,1)S(1)} %get-tuple-element.139, s32[]{:T(128)} %get-tuple-element.136, bf16[4,36864]{1,0:T(4,128)(2,1)} %get-tuple-element.142, s32[]{:T(128)} %bitcast.79), kind=kLoop, calls=%fused_computation.27.clone.1 | loop fusion | bytes 65544 | tf_op jit(solution)/shard_map/vmap()/gather
  5.3 1.4 %bitcast_dynamic-update-slice_fusion.2 = bf16[8,4,4096]{2,1,0:T(4,128)(2,1)S(1)} fusion(bf16[8,4,4096]{2,1,0:T(4,128)(2,1)S(1)} %get-tuple-element.139, s32[]{:T(128)} %get-tuple-element.136, bf16[4,36864]{1,0:T(4,128)(2,1)} %get-tuple-element.142, s32[]{:T(128)} %bitcast.79), kind=kLoop, calls=%fused_computation.27.clone.1 | loop fusion | bytes 65544 | tf_op jit(solution)/shard_map/vmap()/gather
  7.3 1.4 %bitcast_dynamic-update-slice_fusion.2 = bf16[8,4,4096]{2,1,0:T(4,128)(2,1)S(1)} fusion(bf16[8,4,4096]{2,1,0:T(4,128)(2,1)S(1)} %get-tuple-element.139, s32[]{:T(128)} %get-tuple-element.136, bf16[4,36864]{1,0:T(4,128)(2,1)} %get-tuple-element.142, s32[]{:T(128)} %bitcast.79), kind=kLoop, calls=%fused_computation.27.clone.1 | loop fusion | bytes 65544 | tf_op jit(solution)/shard_map/vmap()/gather
  9.3 1.4 %bitcast_dynamic-update-slice_fusion.2 = bf16[8,4,4096]{2,1,0:T(4,128)(2,1)S(1)} fusion(bf16[8,4,4096]{2,1,0:T(4,128)(2,1)S(1)} %get-tuple-element.139, s32[]{:T(128)} %get-tuple-element.136, bf16[4,36864]{1,0:T(4,128)(2,1)} %get-tuple-element.142, s32[]{:T(128)} %bitcast.79), kind=kLoop, calls=%fused_computation.27.clone.1 | loop fusion | bytes 65544 | tf_op jit(solution)/shard_map/vmap()/gather
  11.4 1.4 %bitcast_dynamic-update-slice_fusion.2 = bf16[8,4,4096]{2,1,0:T(4,128)(2,1)S(1)} fusion(bf16[8,4,4096]{2,1,0:T(4,128)(2,1)S(1)} %get-tuple-element.139, s32[]{:T(128)} %get-tuple-element.136, bf16[4,36864]{1,0:T(4,128)(2,1)} %get-tuple-element.142, s32[]{:T(128)} %bitcast.79), kind=kLoop, calls=%fused_computation.27.clone.1 | loop fusion | bytes 65544 | tf_op jit(solution)/shard_map/vmap()/gather
  13.4 1.4 %bitcast_dynamic-update-slice_fusion.2 = bf16[8,4,4096]{2,1,0:T(4,128)(2,1)S(1)} fusion(bf16[8,4,4096]{2,1,0:T(4,128)(2,1)S(1)} %get-tuple-element.139, s32[]{:T(128)} %get-tuple-element.136, bf16[4,36864]{1,0:T(4,128)(2,1)} %get-tuple-element.142, s32[]{:T(128)} %bitcast.79), kind=kLoop, calls=%fused_computation.27.clone.1 | loop fusion | bytes 65544 | tf_op jit(solution)/shard_map/vmap()/gather
  15.4 1.4 %bitcast_dynamic-update-slice_fusion.2 = bf16[8,4,4096]{2,1,0:T(4,128)(2,1)S(1)} fusion(bf16[8,4,4096]{2,1,0:T(4,128)(2,1)S(1)} %get-tuple-element.139, s32[]{:T(128)} %get-tuple-element.136, bf16[4,36864]{1,0:T(4,128)(2,1)} %get-tuple-element.142, s32[]{:T(128)} %bitcast.79), kind=kLoop, calls=%fused_computation.27.clone.1 | loop fusion | bytes 65544 | tf_op jit(solution)/shard_map/vmap()/gather
  16.8 33.9 %negate_convert_fusion = (bf16[4096,512]{1,0:T(8,128)(2,1)S(1)}, bf16[4096,512]{1,0:T(8,128)(2,1)S(1)}) fusion(), kind=kLoop, calls=%fused_computation.39 | loop fusion | flops 35651584 | bytes 8388608 | tf_op jit(solution)/shard_map/convert.7
  50.8 1.6 %multiply_reduce_fusion = (f32[32]{0:T(128)S(1)}, f32[32,1024]{1,0:T(8,128)S(1)}) fusion(bf16[4096,512]{1,0:T(8,128)(2,1)S(1)} %get-tuple-element.73, bf16[4096,512]{1,0:T(8,128)(2,1)S(1)} %get-tuple-element.74, bf16[8,4,4096]{2,1,0:T(4,128)(2,1)S(1)} %get-tuple-element.40), kind=kOutput, calls=%fused_computation.59 | convolution fusion | flops 285278176 | bytes 8781952 | tf_op jit(solution)/shard_map/dot_general | solution.py:32
  52.5 15.7 %all_gather.7 = bf16[16,8,1024]{2,1,0:T(8,128)(2,1)S(1)} all-gather(bf16[4,8,1024]{2,1,0:T(8,128)(2,1)S(1)} %fusion.39), channel_id=1, replica_groups=mesh['group'=2,'src'=4,'rcv'=4] {'src'}, dimensions={0}, use_global_device_ids=true | all-gather | bytes 327680 | tf_op jit(solution)/shard_map/all_gather | solution.py:65
  68.2 1.6 %copy.17 = bf16[16,8,1024]{0,1,2:T(8,128)(2,1)S(1)} copy(bf16[16,8,1024]{2,1,0:T(8,128)(2,1)S(1)} %all_gather.7) | data formatting | bytes 524288 | tf_op jit(solution)/shard_map/while | solution.py:57
  69.8 6.2 %all_gather.6 = bf16[16,8,1024]{2,1,0:T(8,128)(2,1)} all-gather(bf16[4,8,1024]{2,1,0:T(8,128)(2,1)S(1)} %fusion.39), channel_id=1, replica_groups=mesh['group'=2,'src'=4,'rcv'=4] {'rcv'}, dimensions={0}, use_global_device_ids=true | all-gather | bytes 327680 | tf_op jit(solution)/shard_map/all_gather | solution.py:64
  76.1 1.1 cosine_convert_fusion.1
  77.2 0.7 pad_maximum_fusion
  77.9 41.0 %while.11 = (s32[]{:T(128)}, bf16[4,4,16,128]{3,1,0,2:T(4,128)(2,1)}, bf16[4,4,8,1024]{3,2,1,0:T(8,128)(2,1)}, bf16[16,8,1024]{0,1,2:T(8,128)(2,1)S(1)}, bf16[1024,128]{1,0:T(8,128)(2,1)}, /*index=5*/s32[]{:T(128)}) while((s32[]{:T(128)}, bf16[4,4,16,128]{3,1,0,2:T(4,128)(2,1)}, bf16[4,4,8,1024]{3,2,1,0:T(8,128)(2,1)}, ...), condition=%wide.region_2.3_spmd, body=%wide.region_1.2_spmd.sunk | while | flops 19283968 | bytes 4768385 | solution.py:57
  77.9 0.9 constant_dynamic-slice_fusion.4
  78.8 0.7 copy.35
  79.5 0.7 fusion.97
  80.3 1.5 %fusion.99 = bf16[4,16,512]{1,0,2:T(4,128)(2,1)} fusion(f32[512,4,16]{2,1,0:T(4,128)S(1)} %fusion.97, bf16[1,4,8,1024]{2,1,3,0:T(4,128)(2,1)S(1)} %copy.35, bf16[16,8,512]{0,1,2:T(8,128)(2,1)S(1)} %fusion.98), kind=kOutput, calls=%fused_computation.6.clone.2 | convolution fusion | flops 589824 | bytes 393216 | tf_op jit(solution)/shard_map/while/body/eval_jaxpr/sgk,rgk->srk/dot_general | solution.py:45
  81.8 1.9 %copy.37 = bf16[4,16,512]{2,1,0:T(8,128)(2,1)} copy(bf16[4,16,512]{1,0,2:T(4,128)(2,1)} %fusion.99) | data formatting | bytes 131072 | tf_op jit(solution)/shard_map/while/body/eval_jaxpr/add | solution.py:47
  83.8 0.7 fusion.93
  84.6 1.5 %fusion.95 = bf16[4,16,512]{1,0,2:T(4,128)(2,1)} fusion(f32[512,4,16]{2,1,0:T(4,128)S(1)} %fusion.93, bf16[1,4,8,1024]{2,1,3,0:T(4,128)(2,1)S(1)} %copy.35, bf16[16,8,512]{0,1,2:T(8,128)(2,1)S(1)} %fusion.94), kind=kOutput, calls=%fused_computation.5.clone.2 | convolution fusion | flops 589824 | bytes 393216 | tf_op jit(solution)/shard_map/while/body/eval_jaxpr/sgk,rgk->srk/dot_general | solution.py:45
  86.1 1.3 %copy.36 = bf16[4,16,512]{2,1,0:T(8,128)(2,1)S(1)} copy(bf16[4,16,512]{1,0,2:T(4,128)(2,1)} %fusion.95) | data formatting | bytes 131072 | tf_op jit(solution)/shard_map/while/body/eval_jaxpr/sub | solution.py:48
  88.2 0.8 constant_dynamic-slice_fusion.4
  89.8 0.7 fusion.97
  90.5 1.5 %fusion.99 = bf16[4,16,512]{1,0,2:T(4,128)(2,1)} fusion(f32[512,4,16]{2,1,0:T(4,128)S(1)} %fusion.97, bf16[1,4,8,1024]{2,1,3,0:T(4,128)(2,1)S(1)} %copy.35, bf16[16,8,512]{0,1,2:T(8,128)(2,1)S(1)} %fusion.98), kind=kOutput, calls=%fused_computation.6.clone.2 | convolution fusion | flops 589824 | bytes 393216 | tf_op jit(solution)/shard_map/while/body/eval_jaxpr/sgk,rgk->srk/dot_general | solution.py:45
  92.1 1.9 %copy.37 = bf16[4,16,512]{2,1,0:T(8,128)(2,1)} copy(bf16[4,16,512]{1,0,2:T(4,128)(2,1)} %fusion.99) | data formatting | bytes 131072 | tf_op jit(solution)/shard_map/while/body/eval_jaxpr/add | solution.py:47
  94.0 0.7 fusion.93
  94.8 1.5 %fusion.95 = bf16[4,16,512]{1,0,2:T(4,128)(2,1)} fusion(f32[512,4,16]{2,1,0:T(4,128)S(1)} %fusion.93, bf16[1,4,8,1024]{2,1,3,0:T(4,128)(2,1)S(1)} %copy.35, bf16[16,8,512]{0,1,2:T(8,128)(2,1)S(1)} %fusion.94), kind=kOutput, calls=%fused_computation.5.clone.2 | convolution fusion | flops 589824 | bytes 393216 | tf_op jit(solution)/shard_map/while/body/eval_jaxpr/sgk,rgk->srk/dot_general | solution.py:45
  96.4 1.3 %copy.36 = bf16[4,16,512]{2,1,0:T(8,128)(2,1)S(1)} copy(bf16[4,16,512]{1,0,2:T(4,128)(2,1)} %fusion.95) | data formatting | bytes 131072 | tf_op jit(solution)/shard_map/while/body/eval_jaxpr/sub | solution.py:48
  98.4 0.8 constant_dynamic-slice_fusion.4
  100.0 0.7 fusion.97
  100.8 1.5 %fusion.99 = bf16[4,16,512]{1,0,2:T(4,128)(2,1)} fusion(f32[512,4,16]{2,1,0:T(4,128)S(1)} %fusion.97, bf16[1,4,8,1024]{2,1,3,0:T(4,128)(2,1)S(1)} %copy.35, bf16[16,8,512]{0,1,2:T(8,128)(2,1)S(1)} %fusion.98), kind=kOutput, calls=%fused_computation.6.clone.2 | convolution fusion | flops 589824 | bytes 393216 | tf_op jit(solution)/shard_map/while/body/eval_jaxpr/sgk,rgk->srk/dot_general | solution.py:45
  102.3 1.9 %copy.37 = bf16[4,16,512]{2,1,0:T(8,128)(2,1)} copy(bf16[4,16,512]{1,0,2:T(4,128)(2,1)} %fusion.99) | data formatting | bytes 131072 | tf_op jit(solution)/shard_map/while/body/eval_jaxpr/add | solution.py:47
  104.3 0.7 fusion.93
  105.1 1.5 %fusion.95 = bf16[4,16,512]{1,0,2:T(4,128)(2,1)} fusion(f32[512,4,16]{2,1,0:T(4,128)S(1)} %fusion.93, bf16[1,4,8,1024]{2,1,3,0:T(4,128)(2,1)S(1)} %copy.35, bf16[16,8,512]{0,1,2:T(8,128)(2,1)S(1)} %fusion.94), kind=kOutput, calls=%fused_computation.5.clone.2 | convolution fusion | flops 589824 | bytes 393216 | tf_op jit(solution)/shard_map/while/body/eval_jaxpr/sgk,rgk->srk/dot_general | solution.py:45
  106.6 1.3 %copy.36 = bf16[4,16,512]{2,1,0:T(8,128)(2,1)S(1)} copy(bf16[4,16,512]{1,0,2:T(4,128)(2,1)} %fusion.95) | data formatting | bytes 131072 | tf_op jit(solution)/shard_map/while/body/eval_jaxpr/sub | solution.py:48
  108.7 0.8 constant_dynamic-slice_fusion.4
  110.3 0.7 fusion.97
  111.0 1.5 %fusion.99 = bf16[4,16,512]{1,0,2:T(4,128)(2,1)} fusion(f32[512,4,16]{2,1,0:T(4,128)S(1)} %fusion.97, bf16[1,4,8,1024]{2,1,3,0:T(4,128)(2,1)S(1)} %copy.35, bf16[16,8,512]{0,1,2:T(8,128)(2,1)S(1)} %fusion.98), kind=kOutput, calls=%fused_computation.6.clone.2 | convolution fusion | flops 589824 | bytes 393216 | tf_op jit(solution)/shard_map/while/body/eval_jaxpr/sgk,rgk->srk/dot_general | solution.py:45
  112.6 1.9 %copy.37 = bf16[4,16,512]{2,1,0:T(8,128)(2,1)} copy(bf16[4,16,512]{1,0,2:T(4,128)(2,1)} %fusion.99) | data formatting | bytes 131072 | tf_op jit(solution)/shard_map/while/body/eval_jaxpr/add | solution.py:47
  114.6 0.7 fusion.93
  115.3 1.5 %fusion.95 = bf16[4,16,512]{1,0,2:T(4,128)(2,1)} fusion(f32[512,4,16]{2,1,0:T(4,128)S(1)} %fusion.93, bf16[1,4,8,1024]{2,1,3,0:T(4,128)(2,1)S(1)} %copy.35, bf16[16,8,512]{0,1,2:T(8,128)(2,1)S(1)} %fusion.94), kind=kOutput, calls=%fused_computation.5.clone.2 | convolution fusion | flops 589824 | bytes 393216 | tf_op jit(solution)/shard_map/while/body/eval_jaxpr/sgk,rgk->srk/dot_general | solution.py:45
  116.9 1.3 %copy.36 = bf16[4,16,512]{2,1,0:T(8,128)(2,1)S(1)} copy(bf16[4,16,512]{1,0,2:T(4,128)(2,1)} %fusion.95) | data formatting | bytes 131072 | tf_op jit(solution)/shard_map/while/body/eval_jaxpr/sub | solution.py:48
  119.0 1.4 %gather_fusion = bf16[16,16,128]{2,1,0:T(8,128)(2,1)S(1)} fusion(bf16[16,16,128]{2,0,1:T(8,128)(2,1)} %bitcast.80, s32[1024]{0:T(1024)S(1)} %pad_clamp_fusion), kind=kCustom, calls=%fused_computation | custom fusion | bytes 131136 | tf_op jit(solution)/shard_map/jit(_take)/gather | solution.py:66
  (72 shorter events, 11.9 us)
Async XLA Ops:
  77.9 41.0 %copy-start.2 = (s32[1,16]{1,0:T(1,128)S(1)}, s32[1,16]{1,0:T(1,128)}, u32[]{:S(2)}) copy-start(s32[1,16]{1,0:T(1,128)} %param.7) | copy-start | bytes 196
  84.5 2.8 %copy-start = (bf16[1024,128]{1,0:T(8,128)(2,1)S(1)}, bf16[1024,128]{1,0:T(8,128)(2,1)}, u32[]{:S(2)}) copy-start(bf16[1024,128]{1,0:T(8,128)(2,1)} %get-tuple-element.162) | copy-start | bytes 786436 | tf_op jit(solution)/shard_map/while
  84.6 2.8 %copy-start.1 = (bf16[4,16,512]{2,1,0:T(8,128)(2,1)S(1)}, bf16[4,16,512]{2,1,0:T(8,128)(2,1)}, u32[]{:S(2)}) copy-start(bf16[4,16,512]{2,1,0:T(8,128)(2,1)} %copy.37) | copy-start | bytes 196612 | tf_op jit(solution)/shard_map/while
  94.8 2.8 %copy-start = (bf16[1024,128]{1,0:T(8,128)(2,1)S(1)}, bf16[1024,128]{1,0:T(8,128)(2,1)}, u32[]{:S(2)}) copy-start(bf16[1024,128]{1,0:T(8,128)(2,1)} %get-tuple-element.162) | copy-start | bytes 786436 | tf_op jit(solution)/shard_map/while
  94.8 2.8 %copy-start.1 = (bf16[4,16,512]{2,1,0:T(8,128)(2,1)S(1)}, bf16[4,16,512]{2,1,0:T(8,128)(2,1)}, u32[]{:S(2)}) copy-start(bf16[4,16,512]{2,1,0:T(8,128)(2,1)} %copy.37) | copy-start | bytes 196612 | tf_op jit(solution)/shard_map/while
  105.1 2.8 %copy-start = (bf16[1024,128]{1,0:T(8,128)(2,1)S(1)}, bf16[1024,128]{1,0:T(8,128)(2,1)}, u32[]{:S(2)}) copy-start(bf16[1024,128]{1,0:T(8,128)(2,1)} %get-tuple-element.162) | copy-start | bytes 786436 | tf_op jit(solution)/shard_map/while
  105.1 2.8 %copy-start.1 = (bf16[4,16,512]{2,1,0:T(8,128)(2,1)S(1)}, bf16[4,16,512]{2,1,0:T(8,128)(2,1)}, u32[]{:S(2)}) copy-start(bf16[4,16,512]{2,1,0:T(8,128)(2,1)} %copy.37) | copy-start | bytes 196612 | tf_op jit(solution)/shard_map/while
  115.3 2.8 %copy-start = (bf16[1024,128]{1,0:T(8,128)(2,1)S(1)}, bf16[1024,128]{1,0:T(8,128)(2,1)}, u32[]{:S(2)}) copy-start(bf16[1024,128]{1,0:T(8,128)(2,1)} %get-tuple-element.162) | copy-start | bytes 786436 | tf_op jit(solution)/shard_map/while
  115.3 2.8 %copy-start.1 = (bf16[4,16,512]{2,1,0:T(8,128)(2,1)S(1)}, bf16[4,16,512]{2,1,0:T(8,128)(2,1)}, u32[]{:S(2)}) copy-start(bf16[4,16,512]{2,1,0:T(8,128)(2,1)} %copy.37) | copy-start | bytes 196612 | tf_op jit(solution)/shard_map/while
where the time goes:
time: 122 us; the launch traced here: 121 us
  local copies, waits for them, and re-layouts  42.1 us (35%)
  other arithmetic  36.6 us (30%)
  blocking collectives  21.9 us (18%)
  matrix products  20 us (16%)
    another operation x2, other arithmetic  35 us
    dot_general x16, matrix products, pair(): jnp.einsum('sgk,rgk->srk', left, right, preferred_element_type=jnp.float32)  17.6 us
    gather x24, local copies, waits for them, and re-layouts  16 us
    all_gather x1, blocking collectives, on_device(): lax.all_gather(white, 'src', axis=0, tiled=True)  15.7 us
    add x4, local copies, waits for them, and re-layouts, four_sources(): real_part = pair(src_re, rec_re) + pair(src_im, rec_im)  7.62 us
    all_gather x1, blocking collectives, on_device(): sources = lax.all_gather(white, 'rcv', axis=0, tiled=True)  6.23 us
    dynamic_slice x8, local copies, waits for them, and re-layouts, correlate(): out = lax.map(lambda blk: four_sources(blk, receivers, lags), grouped)  6.01 us
    sub x4, local copies, waits for them, and re-layouts, four_sources(): imag_part = pair(src_re, rec_im) - pair(src_im, rec_re)  5.05 us

commit v1 on v0

--- a/solution.py
+++ b/solution.py
@@ -61,7 +61,12 @@
 def on_device(traces, offsets, receiver_slots):
     white = whiten(traces, offsets)
     lags = lag_table()
-    sources = lax.all_gather(white, "rcv", axis=0, tiled=True)
+    ring = [white]
+    for hop in range(3):
+        ring.append(lax.ppermute(ring[-1], "rcv", [(dev, (dev + 1) % 4) for dev in range(4)]))
+    sources = jnp.roll(
+        jnp.concatenate(ring[::-1], axis=0), (lax.axis_index("rcv") + 1) * ring[0].shape[0], axis=0
+    )
     block = correlate(sources, lax.all_gather(white, "src", axis=0, tiled=True), lags)
     return jnp.take(block, receiver_slots[0], axis=1)
 

time: 122 us -> 129 us (1.057)
  blocking collectives: 21.9 us -> 15.7 us
  waiting for transfers between devices: 0 us -> 6.06 us
  matrix products: 20 us -> 22.8 us
  other arithmetic: 36.6 us -> 38.4 us
    all_gather x1 -> x0, blocking collectives: 6.23 us -> none  [on_device(): sources = lax.all_gather(white, 'rcv', axis=0, tiled=True)]
    ppermute x0 -> x3, waiting for transfers between devices: none -> 6.06 us  [on_device(): lax.ppermute(ring[-1], 'rcv', [(dev, (dev + 1) % 4) for dev in range(4)])]
    dot_general x1, matrix products: 1.63 us -> 4.42 us  [whiten(): spectra = jnp.dot(pieces, table, preferred_element_type=jnp.float32)]
  transfers between devices with their start and end apart: 0 -> 3, of which waited for: 0 -> 2; matrix products, arithmetic and copies ran while one was open for 0% -> 4% of each run, Pallas kernels for 0% -> 0%
where the time goes in v1:
time: 129 us; the launch traced here: 127 us
  local copies, waits for them, and re-layouts  43.2 us (33%)
  other arithmetic  38.4 us (30%)
  matrix products  22.8 us (18%)
  blocking collectives  15.7 us (12%)
  waiting for transfers between devices  6.06 us (5%)
    another operation x2, other arithmetic  36.2 us
    dot_general x16, matrix products, pair(): jnp.einsum('sgk,rgk->srk', left, right, preferred_element_type=jnp.float32)  17.7 us
    gather x24, local copies, waits for them, and re-layouts  16.2 us
    all_gather x1, blocking collectives, on_device(): lax.all_gather(white, 'src', axis=0, tiled=True)  15.7 us
    add x4, local copies, waits for them, and re-layouts, four_sources(): real_part = pair(src_re, rec_re) + pair(src_im, rec_im)  7.67 us
    ppermute x3, waiting for transfers between devices, on_device(): lax.ppermute(ring[-1], 'rcv', [(dev, (dev + 1) % 4) for dev in range(4)])  6.06 us
    dynamic_slice x8, local copies, waits for them, and re-layouts, correlate(): out = lax.map(lambda blk: four_sources(blk, receivers, lags), grouped)  6 us
    sub x4, local copies, waits for them, and re-layouts, four_sources(): imag_part = pair(src_re, rec_im) - pair(src_im, rec_re)  5.05 us
  transfers between devices with their start and end apart: 3, of which 2 were waited for; matrix products, arithmetic and copies ran while one was open for 4% of the time, Pallas kernels for 0%

profile of v1, /device:TPU:0, one launch (start us, length us, event | category | flops | bytes accessed | tf_op | source)
XLA Modules:
  0.0 127.5 jit_solution(2804812540017730210)
XLA Ops:
  0.0 35.1 %negate_convert_fusion = (bf16[4096,512]{1,0:T(8,128)(2,1)}, bf16[4096,512]{1,0:T(8,128)(2,1)}) fusion(), kind=kLoop, calls=%fused_computation.39 | loop fusion | flops 35651584 | bytes 8388608 | tf_op jit(solution)/shard_map/convert.7
  35.2 16.3 %while.12 = (s32[]{:T(128)}, bf16[4,36864]{1,0:T(4,128)(2,1)}, s32[8,2]{0,1:T(2,128)S(1)}, bf16[8,4,4096]{2,1,0:T(4,128)(2,1)S(1)}, s32[]{:T(128)}) while((s32[]{:T(128)}, bf16[4,36864]{1,0:T(4,128)(2,1)}, s32[8,2]{0,1:T(2,128)S(1)}, bf16[8,4,4096]{2,1,0:T(4,128)(2,1)S(1)}, s32[]{:T(128)}) %tuple.35), condition=%wide.while_cond, body=%wide.while_body.sunk | while | flops 2 | bytes 65633 | solution.py:30
  35.8 1.4 %bitcast_dynamic-update-slice_fusion.2 = bf16[8,4,4096]{2,1,0:T(4,128)(2,1)S(1)} fusion(bf16[8,4,4096]{2,1,0:T(4,128)(2,1)S(1)} %get-tuple-element.144, s32[]{:T(128)} %get-tuple-element.141, bf16[4,36864]{1,0:T(4,128)(2,1)} %get-tuple-element.147, s32[]{:T(128)} %bitcast.83), kind=kLoop, calls=%fused_computation.27.clone.1 | loop fusion | bytes 65544 | tf_op jit(solution)/shard_map/vmap()/gather
  37.8 1.4 %bitcast_dynamic-update-slice_fusion.2 = bf16[8,4,4096]{2,1,0:T(4,128)(2,1)S(1)} fusion(bf16[8,4,4096]{2,1,0:T(4,128)(2,1)S(1)} %get-tuple-element.144, s32[]{:T(128)} %get-tuple-element.141, bf16[4,36864]{1,0:T(4,128)(2,1)} %get-tuple-element.147, s32[]{:T(128)} %bitcast.83), kind=kLoop, calls=%fused_computation.27.clone.1 | loop fusion | bytes 65544 | tf_op jit(solution)/shard_map/vmap()/gather
  39.8 1.4 %bitcast_dynamic-update-slice_fusion.2 = bf16[8,4,4096]{2,1,0:T(4,128)(2,1)S(1)} fusion(bf16[8,4,4096]{2,1,0:T(4,128)(2,1)S(1)} %get-tuple-element.144, s32[]{:T(128)} %get-tuple-element.141, bf16[4,36864]{1,0:T(4,128)(2,1)} %get-tuple-element.147, s32[]{:T(128)} %bitcast.83), kind=kLoop, calls=%fused_computation.27.clone.1 | loop fusion | bytes 65544 | tf_op jit(solution)/shard_map/vmap()/gather
  41.9 1.4 %bitcast_dynamic-update-slice_fusion.2 = bf16[8,4,4096]{2,1,0:T(4,128)(2,1)S(1)} fusion(bf16[8,4,4096]{2,1,0:T(4,128)(2,1)S(1)} %get-tuple-element.144, s32[]{:T(128)} %get-tuple-element.141, bf16[4,36864]{1,0:T(4,128)(2,1)} %get-tuple-element.147, s32[]{:T(128)} %bitcast.83), kind=kLoop, calls=%fused_computation.27.clone.1 | loop fusion | bytes 65544 | tf_op jit(solution)/shard_map/vmap()/gather
  43.9 1.4 %bitcast_dynamic-update-slice_fusion.2 = bf16[8,4,4096]{2,1,0:T(4,128)(2,1)S(1)} fusion(bf16[8,4,4096]{2,1,0:T(4,128)(2,1)S(1)} %get-tuple-element.144, s32[]{:T(128)} %get-tuple-element.141, bf16[4,36864]{1,0:T(4,128)(2,1)} %get-tuple-element.147, s32[]{:T(128)} %bitcast.83), kind=kLoop, calls=%fused_computation.27.clone.1 | loop fusion | bytes 65544 | tf_op jit(solution)/shard_map/vmap()/gather
  46.0 1.4 %bitcast_dynamic-update-slice_fusion.2 = bf16[8,4,4096]{2,1,0:T(4,128)(2,1)S(1)} fusion(bf16[8,4,4096]{2,1,0:T(4,128)(2,1)S(1)} %get-tuple-element.144, s32[]{:T(128)} %get-tuple-element.141, bf16[4,36864]{1,0:T(4,128)(2,1)} %get-tuple-element.147, s32[]{:T(128)} %bitcast.83), kind=kLoop, calls=%fused_computation.27.clone.1 | loop fusion | bytes 65544 | tf_op jit(solution)/shard_map/vmap()/gather
  48.0 1.4 %bitcast_dynamic-update-slice_fusion.2 = bf16[8,4,4096]{2,1,0:T(4,128)(2,1)S(1)} fusion(bf16[8,4,4096]{2,1,0:T(4,128)(2,1)S(1)} %get-tuple-element.144, s32[]{:T(128)} %get-tuple-element.141, bf16[4,36864]{1,0:T(4,128)(2,1)} %get-tuple-element.147, s32[]{:T(128)} %bitcast.83), kind=kLoop, calls=%fused_computation.27.clone.1 | loop fusion | bytes 65544 | tf_op jit(solution)/shard_map/vmap()/gather
  50.0 1.4 %bitcast_dynamic-update-slice_fusion.2 = bf16[8,4,4096]{2,1,0:T(4,128)(2,1)S(1)} fusion(bf16[8,4,4096]{2,1,0:T(4,128)(2,1)S(1)} %get-tuple-element.144, s32[]{:T(128)} %get-tuple-element.141, bf16[4,36864]{1,0:T(4,128)(2,1)} %get-tuple-element.147, s32[]{:T(128)} %bitcast.83), kind=kLoop, calls=%fused_computation.27.clone.1 | loop fusion | bytes 65544 | tf_op jit(solution)/shard_map/vmap()/gather
  51.5 4.4 %multiply_reduce_fusion = (f32[32]{0:T(128)S(1)}, f32[32,1024]{1,0:T(8,128)S(1)}) fusion(bf16[4096,512]{1,0:T(8,128)(2,1)} %get-tuple-element.78, bf16[4096,512]{1,0:T(8,128)(2,1)} %get-tuple-element.79, bf16[8,4,4096]{2,1,0:T(4,128)(2,1)S(1)} %get-tuple-element.40), kind=kOutput, calls=%fused_computation.59 | convolution fusion | flops 285278176 | bytes 8781952 | tf_op jit(solution)/shard_map/dot_general | solution.py:32
  57.1 1.1 cosine_convert_fusion.1
  58.2 15.7 %all_gather.3 = bf16[16,8,1024]{2,1,0:T(8,128)(2,1)S(1)} all-gather(bf16[4,8,1024]{2,1,0:T(8,128)(2,1)S(1)} %fusion.39), channel_id=1, replica_groups=mesh['group'=2,'src'=4,'rcv'=4] {'src'}, dimensions={0}, use_global_device_ids=true | all-gather | bytes 327680 | tf_op jit(solution)/shard_map/all_gather | solution.py:70
  74.0 1.6 %copy.22 = bf16[16,8,1024]{0,1,2:T(8,128)(2,1)S(1)} copy(bf16[16,8,1024]{2,1,0:T(8,128)(2,1)S(1)} %all_gather.3) | data formatting | bytes 524288 | tf_op jit(solution)/shard_map/while | solution.py:57
  75.7 0.7 pad_maximum_fusion
  76.4 3.0 %collective-permute-done.1 = bf16[4,8,1024]{2,1,0:T(8,128)(2,1)S(1)} collective-permute-done((bf16[4,8,1024]{2,1,0:T(8,128)(2,1)S(1)}, bf16[4,8,1024]{2,1,0:T(8,128)(2,1)S(1)}, u32[]{:S(2)}, u32[]{:S(2)}) %collective-permute-start.1) | collective-permute-done | bytes 65568 | tf_op jit(solution)/shard_map/ppermute | solution.py:66
  80.0 3.1 %collective-permute-done.2 = bf16[4,8,1024]{2,1,0:T(8,128)(2,1)S(1)} collective-permute-done((bf16[4,8,1024]{2,1,0:T(8,128)(2,1)S(1)}, bf16[4,8,1024]{2,1,0:T(8,128)(2,1)S(1)}, u32[]{:S(2)}, u32[]{:S(2)}) %collective-permute-start.2) | collective-permute-done | bytes 65568 | tf_op jit(solution)/shard_map/ppermute | solution.py:66
  83.3 0.7 constant_dynamic-slice_fusion.2
  84.1 41.1 %while.11 = (s32[]{:T(128)}, bf16[4,4,16,128]{3,1,0,2:T(4,128)(2,1)}, bf16[4,4,8,1024]{3,2,1,0:T(8,128)(2,1)}, bf16[16,8,1024]{0,1,2:T(8,128)(2,1)S(1)}, bf16[1024,128]{1,0:T(8,128)(2,1)}, /*index=5*/s32[]{:T(128)}) while((s32[]{:T(128)}, bf16[4,4,16,128]{3,1,0,2:T(4,128)(2,1)}, bf16[4,4,8,1024]{3,2,1,0:T(8,128)(2,1)}, ...), condition=%wide.region_2.3_spmd, body=%wide.region_1.2_spmd.sunk | while | flops 19283968 | bytes 4768385 | solution.py:57
  84.1 0.8 constant_dynamic-slice_fusion.5
  85.6 0.7 fusion.97
  86.4 1.5 %fusion.99 = bf16[4,16,512]{1,0,2:T(4,128)(2,1)} fusion(f32[512,4,16]{2,1,0:T(4,128)S(1)} %fusion.97, bf16[1,4,8,1024]{2,1,3,0:T(4,128)(2,1)S(1)} %copy.40, bf16[16,8,512]{0,1,2:T(8,128)(2,1)S(1)} %fusion.98), kind=kOutput, calls=%fused_computation.6.clone.2 | convolution fusion | flops 589824 | bytes 393216 | tf_op jit(solution)/shard_map/while/body/eval_jaxpr/sgk,rgk->srk/dot_general | solution.py:45
  87.9 1.9 %copy.42 = bf16[4,16,512]{2,1,0:T(8,128)(2,1)} copy(bf16[4,16,512]{1,0,2:T(4,128)(2,1)} %fusion.99) | data formatting | bytes 131072 | tf_op jit(solution)/shard_map/while/body/eval_jaxpr/add | solution.py:47
  89.9 0.7 fusion.93
  90.7 1.5 %fusion.95 = bf16[4,16,512]{1,0,2:T(4,128)(2,1)} fusion(f32[512,4,16]{2,1,0:T(4,128)S(1)} %fusion.93, bf16[1,4,8,1024]{2,1,3,0:T(4,128)(2,1)S(1)} %copy.40, bf16[16,8,512]{0,1,2:T(8,128)(2,1)S(1)} %fusion.94), kind=kOutput, calls=%fused_computation.5.clone.2 | convolution fusion | flops 589824 | bytes 393216 | tf_op jit(solution)/shard_map/while/body/eval_jaxpr/sgk,rgk->srk/dot_general | solution.py:45
  92.2 1.3 copy.41
  94.3 0.8 constant_dynamic-slice_fusion.5
  95.9 0.7 fusion.97
  96.7 1.5 %fusion.99 = bf16[4,16,512]{1,0,2:T(4,128)(2,1)} fusion(f32[512,4,16]{2,1,0:T(4,128)S(1)} %fusion.97, bf16[1,4,8,1024]{2,1,3,0:T(4,128)(2,1)S(1)} %copy.40, bf16[16,8,512]{0,1,2:T(8,128)(2,1)S(1)} %fusion.98), kind=kOutput, calls=%fused_computation.6.clone.2 | convolution fusion | flops 589824 | bytes 393216 | tf_op jit(solution)/shard_map/while/body/eval_jaxpr/sgk,rgk->srk/dot_general | solution.py:45
  98.2 1.9 %copy.42 = bf16[4,16,512]{2,1,0:T(8,128)(2,1)} copy(bf16[4,16,512]{1,0,2:T(4,128)(2,1)} %fusion.99) | data formatting | bytes 131072 | tf_op jit(solution)/shard_map/while/body/eval_jaxpr/add | solution.py:47
  100.2 0.7 fusion.93
  101.0 1.5 %fusion.95 = bf16[4,16,512]{1,0,2:T(4,128)(2,1)} fusion(f32[512,4,16]{2,1,0:T(4,128)S(1)} %fusion.93, bf16[1,4,8,1024]{2,1,3,0:T(4,128)(2,1)S(1)} %copy.40, bf16[16,8,512]{0,1,2:T(8,128)(2,1)S(1)} %fusion.94), kind=kOutput, calls=%fused_computation.5.clone.2 | convolution fusion | flops 589824 | bytes 393216 | tf_op jit(solution)/shard_map/while/body/eval_jaxpr/sgk,rgk->srk/dot_general | solution.py:45
  102.5 1.3 copy.41
  104.6 0.8 constant_dynamic-slice_fusion.5
  106.2 0.7 fusion.97
  107.0 1.5 %fusion.99 = bf16[4,16,512]{1,0,2:T(4,128)(2,1)} fusion(f32[512,4,16]{2,1,0:T(4,128)S(1)} %fusion.97, bf16[1,4,8,1024]{2,1,3,0:T(4,128)(2,1)S(1)} %copy.40, bf16[16,8,512]{0,1,2:T(8,128)(2,1)S(1)} %fusion.98), kind=kOutput, calls=%fused_computation.6.clone.2 | convolution fusion | flops 589824 | bytes 393216 | tf_op jit(solution)/shard_map/while/body/eval_jaxpr/sgk,rgk->srk/dot_general | solution.py:45
  108.5 1.9 %copy.42 = bf16[4,16,512]{2,1,0:T(8,128)(2,1)} copy(bf16[4,16,512]{1,0,2:T(4,128)(2,1)} %fusion.99) | data formatting | bytes 131072 | tf_op jit(solution)/shard_map/while/body/eval_jaxpr/add | solution.py:47
  110.5 0.7 fusion.93
  111.3 1.5 %fusion.95 = bf16[4,16,512]{1,0,2:T(4,128)(2,1)} fusion(f32[512,4,16]{2,1,0:T(4,128)S(1)} %fusion.93, bf16[1,4,8,1024]{2,1,3,0:T(4,128)(2,1)S(1)} %copy.40, bf16[16,8,512]{0,1,2:T(8,128)(2,1)S(1)} %fusion.94), kind=kOutput, calls=%fused_computation.5.clone.2 | convolution fusion | flops 589824 | bytes 393216 | tf_op jit(solution)/shard_map/while/body/eval_jaxpr/sgk,rgk->srk/dot_general | solution.py:45
  112.8 1.3 copy.41
  114.9 0.8 constant_dynamic-slice_fusion.5
  116.5 0.7 fusion.97
  117.3 1.5 %fusion.99 = bf16[4,16,512]{1,0,2:T(4,128)(2,1)} fusion(f32[512,4,16]{2,1,0:T(4,128)S(1)} %fusion.97, bf16[1,4,8,1024]{2,1,3,0:T(4,128)(2,1)S(1)} %copy.40, bf16[16,8,512]{0,1,2:T(8,128)(2,1)S(1)} %fusion.98), kind=kOutput, calls=%fused_computation.6.clone.2 | convolution fusion | flops 589824 | bytes 393216 | tf_op jit(solution)/shard_map/while/body/eval_jaxpr/sgk,rgk->srk/dot_general | solution.py:45
  118.8 1.9 %copy.42 = bf16[4,16,512]{2,1,0:T(8,128)(2,1)} copy(bf16[4,16,512]{1,0,2:T(4,128)(2,1)} %fusion.99) | data formatting | bytes 131072 | tf_op jit(solution)/shard_map/while/body/eval_jaxpr/add | solution.py:47
  120.8 0.7 fusion.93
  121.6 1.5 %fusion.95 = bf16[4,16,512]{1,0,2:T(4,128)(2,1)} fusion(f32[512,4,16]{2,1,0:T(4,128)S(1)} %fusion.93, bf16[1,4,8,1024]{2,1,3,0:T(4,128)(2,1)S(1)} %copy.40, bf16[16,8,512]{0,1,2:T(8,128)(2,1)S(1)} %fusion.94), kind=kOutput, calls=%fused_computation.5.clone.2 | convolution fusion | flops 589824 | bytes 393216 | tf_op jit(solution)/shard_map/while/body/eval_jaxpr/sgk,rgk->srk/dot_general | solution.py:45
  123.1 1.3 copy.41
  125.2 1.5 %gather_fusion = bf16[16,16,128]{2,1,0:T(8,128)(2,1)S(1)} fusion(bf16[16,16,128]{2,0,1:T(8,128)(2,1)} %bitcast.84, s32[1024]{0:T(1024)} %pad_clamp_fusion), kind=kCustom, calls=%fused_computation | custom fusion | bytes 131136 | tf_op jit(solution)/shard_map/jit(_take)/gather | solution.py:71
  (90 shorter events, 14.6 us)
Async XLA Ops:
  0.0 35.1 %copy-start.3 = (s32[8]{0:T(128)S(1)}, s32[8]{0:T(128)}, u32[]{:S(2)}) copy-start(s32[8]{0:T(128)} %param.6) | copy-start | bytes 100
  51.5 5.1 %copy-start.4 = (s32[1,16]{1,0:T(1,128)S(1)}, s32[1,16]{1,0:T(1,128)}, u32[]{:S(2)}) copy-start(s32[1,16]{1,0:T(1,128)} %param.7) | copy-start | bytes 196
  56.0 19.6 %collective-permute-start = (bf16[4,8,1024]{2,1,0:T(8,128)(2,1)S(1)}, bf16[4,8,1024]{2,1,0:T(8,128)(2,1)S(1)}, u32[]{:S(2)}, u32[]{:S(2)}) collective-permute-start(bf16[4,8,1024]{2,1,0:T(8,128)(2,1)S(1)} %fusion.39), channel_id=1, source_target_pairs={{0,1},{1,2},{2,3},{3,0},{4,5},{5,6},{6,7},{7,4},{8,9},{9,10},{10,1... | collective-permute-start | bytes 196616 | tf_op jit(solution)/shard_map/ppermute | solution.py:66
  75.7 3.7 %collective-permute-start.1 = (bf16[4,8,1024]{2,1,0:T(8,128)(2,1)S(1)}, bf16[4,8,1024]{2,1,0:T(8,128)(2,1)S(1)}, u32[]{:S(2)}, u32[]{:S(2)}) collective-permute-start(bf16[4,8,1024]{2,1,0:T(8,128)(2,1)S(1)} %collective-permute-done), channel_id=1, source_target_pairs={{0,1},{1,2},{2,3},{3,0},{4,5},{5,6},{6,7},{7,4},{8,9},{9,10},{10,1... | collective-permute-start | bytes 196616 | tf_op jit(solution)/shard_map/ppermute | solution.py:66
  79.4 3.7 %collective-permute-start.2 = (bf16[4,8,1024]{2,1,0:T(8,128)(2,1)S(1)}, bf16[4,8,1024]{2,1,0:T(8,128)(2,1)S(1)}, u32[]{:S(2)}, u32[]{:S(2)}) collective-permute-start(bf16[4,8,1024]{2,1,0:T(8,128)(2,1)S(1)} %collective-permute-done.1), channel_id=1, source_target_pairs={{0,1},{1,2},{2,3},{3,0},{4,5},{5,6},{6,7},{7,4},{8,9},{9,10},{10,1... | collective-permute-start | bytes 196616 | tf_op jit(solution)/shard_map/ppermute | solution.py:66
  84.1 42.7 %copy-start.2 = (pred[16]{0:T(512)(128)(4,1)S(1)}, pred[16]{0:T(512)(128)(4,1)}, u32[]{:S(2)}) copy-start(pred[16]{0:T(512)(128)(4,1)} %compare_and_fusion) | copy-start | bytes 52
  90.7 2.8 %copy-start = (bf16[1024,128]{1,0:T(8,128)(2,1)S(1)}, bf16[1024,128]{1,0:T(8,128)(2,1)}, u32[]{:S(2)}) copy-start(bf16[1024,128]{1,0:T(8,128)(2,1)} %get-tuple-element.167) | copy-start | bytes 786436 | tf_op jit(solution)/shard_map/while
  90.7 2.8 %copy-start.1 = (bf16[4,16,512]{2,1,0:T(8,128)(2,1)S(1)}, bf16[4,16,512]{2,1,0:T(8,128)(2,1)}, u32[]{:S(2)}) copy-start(bf16[4,16,512]{2,1,0:T(8,128)(2,1)} %copy.42) | copy-start | bytes 196612 | tf_op jit(solution)/shard_map/while
  101.0 2.8 %copy-start = (bf16[1024,128]{1,0:T(8,128)(2,1)S(1)}, bf16[1024,128]{1,0:T(8,128)(2,1)}, u32[]{:S(2)}) copy-start(bf16[1024,128]{1,0:T(8,128)(2,1)} %get-tuple-element.167) | copy-start | bytes 786436 | tf_op jit(solution)/shard_map/while
  101.0 2.8 %copy-start.1 = (bf16[4,16,512]{2,1,0:T(8,128)(2,1)S(1)}, bf16[4,16,512]{2,1,0:T(8,128)(2,1)}, u32[]{:S(2)}) copy-start(bf16[4,16,512]{2,1,0:T(8,128)(2,1)} %copy.42) | copy-start | bytes 196612 | tf_op jit(solution)/shard_map/while
  111.3 2.8 %copy-start = (bf16[1024,128]{1,0:T(8,128)(2,1)S(1)}, bf16[1024,128]{1,0:T(8,128)(2,1)}, u32[]{:S(2)}) copy-start(bf16[1024,128]{1,0:T(8,128)(2,1)} %get-tuple-element.167) | copy-start | bytes 786436 | tf_op jit(solution)/shard_map/while
  111.3 2.8 %copy-start.1 = (bf16[4,16,512]{2,1,0:T(8,128)(2,1)S(1)}, bf16[4,16,512]{2,1,0:T(8,128)(2,1)}, u32[]{:S(2)}) copy-start(bf16[4,16,512]{2,1,0:T(8,128)(2,1)} %copy.42) | copy-start | bytes 196612 | tf_op jit(solution)/shard_map/while
  121.5 2.8 %copy-start = (bf16[1024,128]{1,0:T(8,128)(2,1)S(1)}, bf16[1024,128]{1,0:T(8,128)(2,1)}, u32[]{:S(2)}) copy-start(bf16[1024,128]{1,0:T(8,128)(2,1)} %get-tuple-element.167) | copy-start | bytes 786436 | tf_op jit(solution)/shard_map/while
  121.6 2.8 %copy-start.1 = (bf16[4,16,512]{2,1,0:T(8,128)(2,1)S(1)}, bf16[4,16,512]{2,1,0:T(8,128)(2,1)}, u32[]{:S(2)}) copy-start(bf16[4,16,512]{2,1,0:T(8,128)(2,1)} %copy.42) | copy-start | bytes 196612 | tf_op jit(solution)/shard_map/while
